TPU v7x, 32 devices: a whole 2x2x4 slice. The times are simulated.
32 devices in a mesh: aux: 2 (over x), pair: 16 (over z, y, core).
Axes of the slice: x: 2, y: 2, z: 4, core: 2. Of those that a mesh axis runs over, the one named last changes fastest.
Arguments:
- three_index: bfloat16 [256, 256, 2048], P('pair', None, 'aux'), may hold values from -0.875 to 0.875
- fock_diag: float32 [256], replicated, may hold values from -1.2 to -0.3
- pair_occ: int32 [496, 2], P('pair'), may hold values from 0 to 255, as said below
- pno_count: int32 [496], P('pair'), may hold values from 32 to 128
- pno_energy: float32 [496, 128], P('pair'), may hold values from 0.3 to 3
- pno_coef: bfloat16 [496, 2, 256, 128], P('pair'), may hold values from -0.375 to 0.375
Outputs:
- pair_energy: float32 [496], P('pair')
- grad_ints: float32 [256, 256, 2048], P('pair', None, 'aux')
Inputs may be any that keep to these rules, and one draw needn't show every extreme that they name: `pair_occ`: orbital o belongs to the block o // 16. Among the 62 orbitals named by the pairs of one aligned block of 31 rows, at most 4 belong to any one orbital block, and one orbital block receives exactly 4 from every such row block; i may equal j.
All inputs are finite; a program needn't handle non-finite values.
Results may differ from a plain program's by a relative error of at most 0.0061.
Values may be sent and summed in bfloat16 or wider, within the bound.
No kernel may reach another device: no remote copies, remote signals or barrier semaphores. Data moves between devices by JAX's collectives and lax.ppermute only.
A program may use at most 128 MiB of HBM per device.

v0:
```python
import jax
import jax.numpy as jnp
from jax import lax
from jax.sharding import PartitionSpec as P


def local(three_index, fock_diag, pair_occ, pno_count, pno_energy, pno_coef):
    groups = lax.axis_size("pair")
    occ_dev = three_index.shape[0]
    width_dom = three_index.shape[1]
    width_aux = three_index.shape[2]
    pair_dev = pair_occ.shape[0]
    width_pno = pno_coef.shape[3]
    halves = 2 * pair_dev
    capacity = max(2, halves // groups + 1)
    slots = groups * capacity
    occ_flat = pair_occ.reshape(halves)
    owner_of = occ_flat // occ_dev
    local_index = occ_flat % occ_dev
    owner_hot = (owner_of[:, None] == jnp.arange(groups, dtype=jnp.int32)[None, :]).astype(
        jnp.int32
    )
    before = jnp.cumsum(owner_hot, axis=0) - owner_hot
    rank_in = jnp.sum(before * owner_hot, axis=1)
    slot_of = owner_of * capacity + rank_in
    request = jnp.zeros((slots,), jnp.int32).at[slot_of].set(local_index + 1)
    arrived = lax.all_to_all(
        request.reshape(groups, capacity), "pair", split_axis=0, concat_axis=0, tiled=True
    ).reshape(slots)
    is_live = arrived > 0
    row_index = jnp.maximum(arrived - 1, 0)
    selected = jnp.take(three_index, row_index, axis=0)
    selected = jnp.where(is_live[:, None, None], selected, jnp.zeros_like(selected))
    coef_half = pno_coef.reshape(halves, width_dom, width_pno)
    coef_send = jnp.zeros((slots, width_dom, width_pno), jnp.bfloat16).at[slot_of].set(coef_half)
    coef_recv = lax.all_to_all(
        coef_send.reshape(groups, capacity, width_dom, width_pno),
        "pair",
        split_axis=0,
        concat_axis=0,
        tiled=True,
    )
    coef_recv = coef_recv.reshape(slots, width_dom, width_pno)
    proj_here = jnp.einsum(
        "sdp,sdq->spq", coef_recv, selected, preferred_element_type=jnp.float32
    ).astype(jnp.bfloat16)
    proj_back = lax.all_to_all(
        proj_here.reshape(groups, capacity, width_pno, width_aux),
        "pair",
        split_axis=0,
        concat_axis=0,
        tiled=True,
    )
    projected = jnp.take(proj_back.reshape(slots, width_pno, width_aux), slot_of, axis=0)
    paired = projected.reshape(pair_dev, 2, width_pno, width_aux)
    rows_i = paired[:, 0]
    rows_j = paired[:, 1]
    partial_sum = jnp.einsum("kpq,krq->kpr", rows_i, rows_j, preferred_element_type=jnp.float32)
    coupling = lax.psum(partial_sum, "aux")
    fock_i = jnp.take(fock_diag, pair_occ[:, 0])
    fock_j = jnp.take(fock_diag, pair_occ[:, 1])
    denom = pno_energy[:, :, None] + pno_energy[:, None, :] - (fock_i + fock_j)[:, None, None]
    in_pno = jnp.arange(width_pno, dtype=jnp.int32)[None, :] < pno_count[:, None]
    both_in = in_pno[:, :, None] & in_pno[:, None, :]
    amplitude = jnp.where(both_in, -coupling / denom, jnp.float32(0.0))
    mixed = 2.0 * amplitude - jnp.swapaxes(amplitude, 1, 2)
    energy = jnp.sum(coupling * mixed, axis=(1, 2)) / (width_pno * width_pno)
    weights = mixed.astype(jnp.bfloat16)
    gamma_i = jnp.einsum(
        "kab,kbq->kaq", weights, rows_j, preferred_element_type=jnp.float32
    ).astype(jnp.bfloat16)
    gamma_j = jnp.einsum(
        "kba,kbq->kaq", weights, rows_i, preferred_element_type=jnp.float32
    ).astype(jnp.bfloat16)
    gamma = jnp.stack([gamma_i, gamma_j], axis=1).reshape(halves, width_pno, width_aux)
    gamma_send = jnp.zeros((slots, width_pno, width_aux), jnp.bfloat16).at[slot_of].set(gamma)
    gamma_recv = lax.all_to_all(
        gamma_send.reshape(groups, capacity, width_pno, width_aux),
        "pair",
        split_axis=0,
        concat_axis=0,
        tiled=True,
    )
    gamma_recv = gamma_recv.reshape(slots, width_pno, width_aux)
    terms = jnp.einsum(
        "sdp,spq->sdq", coef_recv, gamma_recv, preferred_element_type=jnp.float32
    ).astype(jnp.bfloat16)
    occ_hot = (row_index[None, :] == jnp.arange(occ_dev, dtype=jnp.int32)[:, None]) & is_live[
        None, :
    ]
    grad = jnp.dot(
        occ_hot.astype(jnp.bfloat16),
        terms.reshape(slots, width_dom * width_aux),
        preferred_element_type=jnp.float32,
    )
    return (energy, grad.reshape(occ_dev, width_dom, width_aux))


def solution(mesh):
    placed = (
        P("pair", None, "aux"),
        P(),
        P("pair", None),
        P("pair"),
        P("pair", None),
        P("pair", None, None, None),
    )
    return jax.shard_map(
        local,
        mesh=mesh,
        in_specs=placed,
        out_specs=(P("pair"), P("pair", None, "aux")),
        check_vma=False,
    )
```

profile of v0, /device:TPU:13, one launch (start us, length us, event | category | flops | bytes accessed | tf_op | source)
XLA Modules:
  0.0 1180.7 jit_solution(13151449799421802586)
XLA Ops:
  7.2 0.8 copy.53
  8.6 0.8 scatter_custom_fusion.1
  10.0 6.5 all-to-all-start.1
  16.5 3.0 broadcast_in_dim.61
  19.6 11.7 scatter_fusion
  31.3 6.4 copy.56
  37.7 6.0 all-to-all-start
  44.0 15.7 %gather_fusion = bf16[64,256,1024]{2,1,0:T(8,128)(2,1)} fusion(bf16[16,256,1024]{2,1,0:T(8,128)(2,1)} %param.8, s32[1024]{0:T(1024)S(1)} %pad_clamp_fusion.3), kind=kCustom, calls=%fused_computation.2 | custom fusion | bytes 67109120 | tf_op jit(solution)/shard_map/jit(_take)/gather | solution.py:32
  59.7 76.5 %all-to-all-done = bf16[16,4,256,128]{2,3,1,0:T(8,128)(2,1)} async-done(((bf16[16,4,256,128]{2,3,1,0:T(8,128)(2,1)}), bf16[16,4,256,128]{2,3,1,0:T(8,128)(2,1)}, u32[]{:S(2)}, u32[]{:S(2)}) %all-to-all-start) | async-done | bytes 4194336 | tf_op jit(solution)/shard_map/all_to_all | solution.py:36
  136.2 18.3 %fusion.10 = bf16[64,128,1024]{2,1,0:T(8,128)(2,1)} fusion(bf16[64,256,128]{1,2,0:T(8,128)(2,1)} %bitcast.4, bf16[64,256,1024]{2,1,0:T(8,128)(2,1)} %gather_fusion, pred[64]{0:T(512)(128)(4,1)S(1)} %broadcast_compare_fusion, pred[64]{0:T(512)(128)(4,1)S(1)} %gt.15), kind=kOutput, calls=%fused_computation.20 | convolution fusion | flops 4336910336 | bytes 54526080 | tf_op jit(solution)/shard_map/sdp,sdq->spq/dot_general | solution.py:44
  154.5 5.2 all-to-all-start.2
  160.1 361.4 %all-to-all-done.2 = bf16[16,4,128,1024]{3,2,1,0:T(8,128)(2,1)} async-done(((bf16[16,4,128,1024]{3,2,1,0:T(8,128)(2,1)}), bf16[16,4,128,1024]{3,2,1,0:T(8,128)(2,1)}, u32[]{:S(2)}, u32[]{:S(2)}) %all-to-all-start.2) | async-done | bytes 16777248 | tf_op jit(solution)/shard_map/all_to_all | solution.py:47
  521.5 13.3 %gather_fusion.1 = bf16[62,128,1024]{2,1,0:T(8,128)(2,1)} fusion(bf16[64,128,1024]{2,1,0:T(8,128)(2,1)} %bitcast.7, s32[1024]{0:T(1024)S(1)} %pad_clamp_fusion.2), kind=kCustom, calls=%fused_computation.3 | custom fusion | bytes 32506104 | tf_op jit(solution)/shard_map/jit(_take)/gather | solution.py:54
  534.8 13.8 %copy_select_fusion = bf16[31,2,128,1024]{3,2,0,1:T(8,128)(2,1)} fusion(bf16[31,2,128,1024]{3,2,1,0:T(8,128)(2,1)} %bitcast.68, pred[31,2]{0,1:T(4,128)(4,1)S(1)} %compare_and_fusion), kind=kLoop, calls=%fused_computation.19 | loop fusion | flops 8126464 | bytes 32505918 | tf_op jit(solution)/shard_map/jit(_take)/select_n | solution.py:54
  548.7 9.2 fusion.14
  558.0 0.7 gather_fusion.2
  559.5 59.4 %all-reduce.2.cloned.1.call-done = f32[31,128,128]{2,1,0:T(8,128)} async-done(((f32[31,128,128]{2,1,0:T(8,128)}), f32[31,128,128]{2,1,0:T(8,128)}) %all-reduce.2.cloned.1.call-update) | async-done | bytes 2031632 | tf_op jit(solution)/shard_map/psum | solution.py:59
  618.9 2.3 copy.59
  621.2 2.6 broadcast_multiply_fusion
  623.9 2.9 copy.60
  626.7 3.8 fusion.16
  630.5 5.6 convert_bitcast_fusion.1
  636.1 8.9 convert_bitcast_fusion
  645.0 6.2 pad_maximum_fusion
  651.2 6.4 copy.62
  657.6 6.1 broadcast_in_dim.68
  663.7 41.4 %scatter_fusion.1 = bf16[64,128,1024]{2,1,0:T(8,128)(2,1)} fusion(bf16[64,128,1024]{2,1,0:T(8,128)(2,1)} %broadcast_in_dim.68, s32[62]{0:T(128)S(1)} %fusion.25, bf16[62,128,1024]{2,1,0:T(8,128)(2,1)} %bitcast.67), kind=kCustom, calls=%fused_computation.6 | custom fusion | bytes 48759032 | tf_op jit(solution)/shard_map/scatter | solution.py:76
  705.1 6.5 all-to-all-start.3
  712.1 361.6 %all-to-all-done.3 = bf16[16,4,128,1024]{3,2,1,0:T(8,128)(2,1)} async-done(((bf16[16,4,128,1024]{3,2,1,0:T(8,128)(2,1)}), bf16[16,4,128,1024]{3,2,1,0:T(8,128)(2,1)}, u32[]{:S(2)}, u32[]{:S(2)}) %all-to-all-start.3) | async-done | bytes 16777248 | tf_op jit(solution)/shard_map/all_to_all | solution.py:77
  1073.7 21.3 %convolution_convert_fusion = bf16[64,256,1024]{2,1,0:T(8,128)(2,1)} fusion(bf16[64,256,128]{1,2,0:T(8,128)(2,1)} %bitcast.4, bf16[64,128,1024]{2,1,0:T(8,128)(2,1)} %bitcast.19), kind=kOutput, calls=%fused_computation.15 | convolution fusion | flops 4311744512 | bytes 54525952 | tf_op jit(solution)/shard_map/sdp,spq->sdq/dot_general | solution.py:85
  1095.0 60.6 %fusion = f32[16,256,1024]{2,0,1:T(8,128)} fusion(s32[64]{0:T(128)S(1)} %max.23, pred[64]{0:T(512)(128)(4,1)S(1)} %gt.15, bf16[8,8,256,1024]{3,2,1,0:T(8,128)(2,1)} %bitcast.65), kind=kOutput, calls=%fused_computation.7 | convolution fusion | flops 536872960 | bytes 50331968 | tf_op jit(solution)/shard_map/dot_general | solution.py:91
  1155.6 17.8 %copy.65 = f32[16,256,1024]{2,1,0:T(8,128)} copy(f32[16,256,1024]{2,0,1:T(8,128)} %fusion) | data formatting | bytes 33554432
  (37 shorter events, 3.3 us)
Async XLA Ops:
  7.2 550.8 %copy-start = (f32[256]{0:T(256)S(1)}, f32[256]{0:T(256)}, u32[]{:S(2)}) copy-start(f32[256]{0:T(256)} %param.9) | copy-start | bytes 3076
  10.0 27.7 %all-to-all-start.1 = ((s32[16,1,4]{2,1,0:T(1,128)}), s32[16,1,4]{2,1,0:T(1,128)S(1)}, u32[]{:S(2)}, u32[]{:S(2)}) async-start(s32[16,1,4]{2,1,0:T(1,128)} %bitcast.5), calls=%async_computation.1 | async-start | bytes 16384 | tf_op jit(solution)/shard_map/all_to_all | solution.py:27
  37.7 98.5 %all-to-all-start = ((bf16[16,4,256,128]{2,3,1,0:T(8,128)(2,1)}), bf16[16,4,256,128]{2,3,1,0:T(8,128)(2,1)}, u32[]{:S(2)}, u32[]{:S(2)}) async-start(bf16[16,4,256,128]{2,3,1,0:T(8,128)(2,1)} %copy.56), calls=%async_computation | async-start | bytes 8388608 | tf_op jit(solution)/shard_map/all_to_all | solution.py:36
  154.5 5.6 copy-start.3
  154.5 367.0 %all-to-all-start.2 = ((bf16[16,4,128,1024]{3,2,1,0:T(8,128)(2,1)}), bf16[16,4,128,1024]{3,2,1,0:T(8,128)(2,1)}, u32[]{:S(2)}, u32[]{:S(2)}) async-start(bf16[16,4,128,1024]{3,2,1,0:T(8,128)(2,1)} %bitcast.70), calls=%async_computation.2 | async-start | bytes 33554432 | tf_op jit(solution)/shard_map/all_to_all | solution.py:47
  159.6 459.2 %all-reduce.2.cloned.1.call-start = ((), (), s32[]{:S(2)}) async-start(), calls=%async_computation.4 | async-start | bytes 4063232 | tf_op jit(solution)/shard_map/psum | solution.py:59
  548.7 10.7 copy-start.4
  548.7 72.5 %copy-start.2 = (f32[31,128]{1,0:T(8,128)S(1)}, f32[31,128]{1,0:T(8,128)}, u32[]{:S(2)}) copy-start(f32[31,128]{1,0:T(8,128)} %param.12) | copy-start | bytes 47620
  705.1 368.6 %all-to-all-start.3 = ((bf16[16,4,128,1024]{3,2,1,0:T(8,128)(2,1)}), bf16[16,4,128,1024]{3,2,1,0:T(8,128)(2,1)}, u32[]{:S(2)}, u32[]{:S(2)}) async-start(bf16[16,4,128,1024]{3,2,1,0:T(8,128)(2,1)} %bitcast.66), calls=%async_computation.3 | async-start | bytes 33554432 | tf_op jit(solution)/shard_map/all_to_all | solution.py:77
  1095.0 78.3 %copy-start.1 = (f32[256]{0:T(256)S(1)}, f32[256]{0:T(256)}, u32[]{:S(2)}) copy-start(f32[256]{0:T(256)} %param.9) | copy-start | bytes 3076
Sparse Core Ops, SparseCore 0:
  558.1 60.7 all-reduce.1
where the time goes:
time: 1190 us; the launch traced here: 1180 us
  waiting for transfers between devices  859 us (72%)
  local copies, waits for them, and re-layouts  131 us (11%)
  matrix products  124 us (10%)
  other arithmetic  27.5 us (2%)
  starting transfers between devices  24.4 us (2%)
  between operations  14.6 us (1%)
    all_to_all x1, waiting for transfers between devices, local(): lax.all_to_all(gamma_send.reshape(groups, capacity, width_pno, width_aux)...  362 us
    all_to_all x1, waiting for transfers between devices, local(): lax.all_to_all(proj_here.reshape(groups, capacity, width_pno, width_aux),...  361 us
    all_to_all x1, waiting for transfers between devices, local(): lax.all_to_all(coef_send.reshape(groups, capacity, width_dom, width_pno),...  76.5 us
    dot_general x1, matrix products, local(): jnp.dot(occ_hot.astype(jnp.bfloat16), terms.reshape(slots, width_dom * wi...  60.6 us
    psum x1, waiting for transfers between devices, local(): coupling = lax.psum(partial_sum, 'aux')  59.4 us
    scatter x1, local copies, waits for them, and re-layouts, local(): jnp.zeros((slots, width_pno, width_aux), jnp.bfloat16).at[slot_of]  41.4 us
  transfers between devices with their start and end apart: 5, of which 4 were waited for; matrix products, arithmetic and copies ran while one was open for 3% of the time, Pallas kernels for 0%

commit v1 on v0

--- a/solution.py
+++ b/solution.py
@@ -56,7 +56,7 @@
     rows_i = paired[:, 0]
     rows_j = paired[:, 1]
     partial_sum = jnp.einsum("kpq,krq->kpr", rows_i, rows_j, preferred_element_type=jnp.float32)
-    coupling = lax.psum(partial_sum, "aux")
+    coupling = jax.lax.all_gather(partial_sum, axis_name="aux").sum(axis=0)
     fock_i = jnp.take(fock_diag, pair_occ[:, 0])
     fock_j = jnp.take(fock_diag, pair_occ[:, 1])
     denom = pno_energy[:, :, None] + pno_energy[:, None, :] - (fock_i + fock_j)[:, None, None]

time: 1190 us -> 1180 us (level)
    psum x1 -> x0, waiting for transfers between devices: 59.4 us -> none  [local(): coupling = lax.psum(partial_sum, 'aux')]
    all_gather x0 -> x1, waiting for transfers between devices: none -> 53.1 us  [local(): coupling = jax.lax.all_gather(partial_sum, axis_name='aux').sum(axis=0)]
where the time goes in v1:
time: 1180 us
  waiting for transfers between devices  853 us (72%)
  local copies, waits for them, and re-layouts  131 us (11%)
  matrix products  124 us (11%)
  other arithmetic  30.8 us (3%)
  starting transfers between devices  24.4 us (2%)
  between operations  14.6 us (1%)
    all_to_all x1, waiting for transfers between devices, local(): lax.all_to_all(gamma_send.reshape(groups, capacity, width_pno, width_aux)...  362 us
    all_to_all x1, waiting for transfers between devices, local(): lax.all_to_all(proj_here.reshape(groups, capacity, width_pno, width_aux),...  361 us
    all_to_all x1, waiting for transfers between devices, local(): lax.all_to_all(coef_send.reshape(groups, capacity, width_dom, width_pno),...  76.4 us
    dot_general x1, matrix products, local(): jnp.dot(occ_hot.astype(jnp.bfloat16), terms.reshape(slots, width_dom * wi...  60.6 us
    all_gather x1, waiting for transfers between devices, local(): coupling = jax.lax.all_gather(partial_sum, axis_name='aux').sum(axis=0)  53.1 us
    scatter x1, local copies, waits for them, and re-layouts, local(): jnp.zeros((slots, width_pno, width_aux), jnp.bfloat16).at[slot_of]  41.4 us
  transfers between devices with their start and end apart: 5, of which 4 were waited for; matrix products, arithmetic and copies ran while one was open for 3% of the time, Pallas kernels for 0%

profile of v1, /device:TPU:13, one launch (start us, length us, event | category | flops | bytes accessed | tf_op | source)
XLA Modules:
  0.0 1177.3 jit_solution(12864915644285805620)
XLA Ops:
  7.2 0.8 copy.55
  8.6 0.8 scatter_custom_fusion.1
  10.0 6.5 all-to-all-start.1
  16.5 3.0 broadcast_in_dim.61
  19.6 11.7 scatter_fusion
  31.3 6.4 copy.58
  37.7 6.0 all-to-all-start
  44.0 15.7 %gather_fusion = bf16[64,256,1024]{2,1,0:T(8,128)(2,1)} fusion(bf16[16,256,1024]{2,1,0:T(8,128)(2,1)} %param.8, s32[1024]{0:T(1024)S(1)} %pad_clamp_fusion.3), kind=kCustom, calls=%fused_computation.2 | custom fusion | bytes 67109120 | tf_op jit(solution)/shard_map/jit(_take)/gather | solution.py:32
  59.7 76.4 %all-to-all-done = bf16[16,4,256,128]{2,3,1,0:T(8,128)(2,1)} async-done(((bf16[16,4,256,128]{2,3,1,0:T(8,128)(2,1)}), bf16[16,4,256,128]{2,3,1,0:T(8,128)(2,1)}, u32[]{:S(2)}, u32[]{:S(2)}) %all-to-all-start) | async-done | bytes 4194336 | tf_op jit(solution)/shard_map/all_to_all | solution.py:36
  136.2 18.3 %fusion.10 = bf16[64,128,1024]{2,1,0:T(8,128)(2,1)} fusion(bf16[64,256,128]{1,2,0:T(8,128)(2,1)} %bitcast.4, bf16[64,256,1024]{2,1,0:T(8,128)(2,1)} %gather_fusion, pred[64]{0:T(512)(128)(4,1)S(1)} %broadcast_compare_fusion, pred[64]{0:T(512)(128)(4,1)S(1)} %gt.15), kind=kOutput, calls=%fused_computation.20 | convolution fusion | flops 4336910336 | bytes 54526080 | tf_op jit(solution)/shard_map/sdp,sdq->spq/dot_general | solution.py:44
  154.5 5.2 all-to-all-start.2
  160.1 361.4 %all-to-all-done.2 = bf16[16,4,128,1024]{3,2,1,0:T(8,128)(2,1)} async-done(((bf16[16,4,128,1024]{3,2,1,0:T(8,128)(2,1)}), bf16[16,4,128,1024]{3,2,1,0:T(8,128)(2,1)}, u32[]{:S(2)}, u32[]{:S(2)}) %all-to-all-start.2) | async-done | bytes 16777248 | tf_op jit(solution)/shard_map/all_to_all | solution.py:47
  521.5 13.3 %gather_fusion.1 = bf16[62,128,1024]{2,1,0:T(8,128)(2,1)} fusion(bf16[64,128,1024]{2,1,0:T(8,128)(2,1)} %bitcast.7, s32[1024]{0:T(1024)S(1)} %pad_clamp_fusion.2), kind=kCustom, calls=%fused_computation.3 | custom fusion | bytes 32506104 | tf_op jit(solution)/shard_map/jit(_take)/gather | solution.py:54
  534.8 13.8 %copy_select_fusion = bf16[31,2,128,1024]{3,2,0,1:T(8,128)(2,1)} fusion(bf16[31,2,128,1024]{3,2,1,0:T(8,128)(2,1)} %bitcast.68, pred[31,2]{0,1:T(4,128)(4,1)S(1)} %compare_and_fusion), kind=kLoop, calls=%fused_computation.19 | loop fusion | flops 8126464 | bytes 32505918 | tf_op jit(solution)/shard_map/jit(_take)/select_n | solution.py:54
  548.7 9.2 fusion.14
  559.5 53.1 %all-gather.3.cloned.1.call-done = f32[62,128,128]{2,1,0:T(8,128)} async-done(((f32[31,128,128]{2,1,0:T(8,128)}), f32[62,128,128]{2,1,0:T(8,128)}) %all-gather.3.cloned.1.call-update) | async-done | bytes 4063248 | tf_op jit(solution)/shard_map/all_gather | solution.py:59
  612.6 2.7 reduce_sum.34
  615.3 2.1 copy.61
  617.4 3.1 neg.7
  620.5 2.9 copy.62
  623.4 3.8 multiply_reduce_fusion
  627.2 5.6 convert_bitcast_fusion.1
  632.8 8.9 convert_bitcast_fusion
  641.7 6.2 pad_maximum_fusion
  647.9 6.4 copy.64
  654.3 6.1 broadcast_in_dim.68
  660.4 41.4 %scatter_fusion.1 = bf16[64,128,1024]{2,1,0:T(8,128)(2,1)} fusion(bf16[64,128,1024]{2,1,0:T(8,128)(2,1)} %broadcast_in_dim.68, s32[62]{0:T(128)S(1)} %fusion.28, bf16[62,128,1024]{2,1,0:T(8,128)(2,1)} %bitcast.67), kind=kCustom, calls=%fused_computation.6 | custom fusion | bytes 48759032 | tf_op jit(solution)/shard_map/scatter | solution.py:76
  701.7 6.5 all-to-all-start.3
  708.8 361.6 %all-to-all-done.3 = bf16[16,4,128,1024]{3,2,1,0:T(8,128)(2,1)} async-done(((bf16[16,4,128,1024]{3,2,1,0:T(8,128)(2,1)}), bf16[16,4,128,1024]{3,2,1,0:T(8,128)(2,1)}, u32[]{:S(2)}, u32[]{:S(2)}) %all-to-all-start.3) | async-done | bytes 16777248 | tf_op jit(solution)/shard_map/all_to_all | solution.py:77
  1070.4 21.3 %convolution_convert_fusion = bf16[64,256,1024]{2,1,0:T(8,128)(2,1)} fusion(bf16[64,256,128]{1,2,0:T(8,128)(2,1)} %bitcast.4, bf16[64,128,1024]{2,1,0:T(8,128)(2,1)} %bitcast.20), kind=kOutput, calls=%fused_computation.15 | convolution fusion | flops 4311744512 | bytes 54525952 | tf_op jit(solution)/shard_map/sdp,spq->sdq/dot_general | solution.py:85
  1091.7 60.6 %fusion = f32[16,256,1024]{2,0,1:T(8,128)} fusion(s32[64]{0:T(128)S(1)} %copy-done.5, pred[64]{0:T(512)(128)(4,1)S(1)} %gt.15, bf16[8,8,256,1024]{3,2,1,0:T(8,128)(2,1)} %bitcast.65), kind=kOutput, calls=%fused_computation.7 | convolution fusion | flops 536872960 | bytes 50331968 | tf_op jit(solution)/shard_map/dot_general | solution.py:91
  1152.3 17.8 %copy.67 = f32[16,256,1024]{2,1,0:T(8,128)} copy(f32[16,256,1024]{2,0,1:T(8,128)} %fusion) | data formatting | bytes 33554432
  (42 shorter events, 4.0 us)
Async XLA Ops:
  7.2 550.8 %copy-start = (f32[256]{0:T(256)S(1)}, f32[256]{0:T(256)}, u32[]{:S(2)}) copy-start(f32[256]{0:T(256)} %param.9) | copy-start | bytes 3076
  10.0 27.7 %all-to-all-start.1 = ((s32[16,1,4]{2,1,0:T(1,128)}), s32[16,1,4]{2,1,0:T(1,128)S(1)}, u32[]{:S(2)}, u32[]{:S(2)}) async-start(s32[16,1,4]{2,1,0:T(1,128)} %bitcast.5), calls=%async_computation.1 | async-start | bytes 16384 | tf_op jit(solution)/shard_map/all_to_all | solution.py:27
  37.7 98.5 %all-to-all-start = ((bf16[16,4,256,128]{2,3,1,0:T(8,128)(2,1)}), bf16[16,4,256,128]{2,3,1,0:T(8,128)(2,1)}, u32[]{:S(2)}, u32[]{:S(2)}) async-start(bf16[16,4,256,128]{2,3,1,0:T(8,128)(2,1)} %copy.58), calls=%async_computation | async-start | bytes 8388608 | tf_op jit(solution)/shard_map/all_to_all | solution.py:36
  43.8 15.9 %copy-start.4 = (s32[64]{0:T(128)}, s32[64]{0:T(128)S(1)}, u32[]{:S(2)}) copy-start(s32[64]{0:T(128)S(1)} %max.23) | copy-start | bytes 772
  154.5 5.6 copy-start.3
  154.5 367.0 %all-to-all-start.2 = ((bf16[16,4,128,1024]{3,2,1,0:T(8,128)(2,1)}), bf16[16,4,128,1024]{3,2,1,0:T(8,128)(2,1)}, u32[]{:S(2)}, u32[]{:S(2)}) async-start(bf16[16,4,128,1024]{3,2,1,0:T(8,128)(2,1)} %bitcast.70), calls=%async_computation.2 | async-start | bytes 33554432 | tf_op jit(solution)/shard_map/all_to_all | solution.py:47
  159.7 452.9 %all-gather.3.cloned.1.call-start = ((), (), s32[]{:S(2)}) async-start(), calls=%async_computation.4 | async-start | bytes 6094848 | tf_op jit(solution)/shard_map/all_gather | solution.py:59
  548.7 10.7 copy-start.6
  557.9 65.5 %copy-start.2 = (f32[31,128]{1,0:T(8,128)S(1)}, f32[31,128]{1,0:T(8,128)}, u32[]{:S(2)}) copy-start(f32[31,128]{1,0:T(8,128)} %param.12) | copy-start | bytes 47620
  701.7 368.6 %all-to-all-start.3 = ((bf16[16,4,128,1024]{3,2,1,0:T(8,128)(2,1)}), bf16[16,4,128,1024]{3,2,1,0:T(8,128)(2,1)}, u32[]{:S(2)}, u32[]{:S(2)}) async-start(bf16[16,4,128,1024]{3,2,1,0:T(8,128)(2,1)} %bitcast.66), calls=%async_computation.3 | async-start | bytes 33554432 | tf_op jit(solution)/shard_map/all_to_all | solution.py:77
  1070.4 21.3 %copy-start.5 = (s32[64]{0:T(128)S(1)}, s32[64]{0:T(128)}, u32[]{:S(2)}) copy-start(s32[64]{0:T(128)} %copy-done.4) | copy-start | bytes 772
  1091.7 78.4 %copy-start.1 = (f32[256]{0:T(256)S(1)}, f32[256]{0:T(256)}, u32[]{:S(2)}) copy-start(f32[256]{0:T(256)} %param.9) | copy-start | bytes 3076
Sparse Core Ops, SparseCore 0:
  558.0 54.4 all-gather.2
